TPU v7x, 32 devices: a whole 2x2x4 slice. The times are simulated.
32 devices in a mesh: expert: 8 (over z, y), dp: 4 (over x, core).
Axes of the slice: x: 2, y: 2, z: 4, core: 2. Of those that a mesh axis runs over, the one named last changes fastest.
Arguments:
- tokens_t: bfloat16 [7168, 512], P('expert', 'dp'), may hold values from -6 to 6
- slot_row: int32 [4, 1024], P('dp'), may hold values from -1 to 127, as said below
- slot_gate: float32 [4, 1024], P('dp'), may hold values from 0.2 to 1
- block_hot: int32 [4, 8], P('dp'), may hold values from 0 to 1, as said below
- hot_owner: int32 [1], replicated, may hold values from 0 to 255
- w_in: bfloat16 [4, 2, 2048, 7168], P('dp', None, 'expert'), may hold values from -0.0625 to 0.0625
- w_out: bfloat16 [4, 7168, 2048], P('dp', None, 'expert'), may hold values from -0.125 to 0.125
Outputs:
- mixed_t: bfloat16 [7168, 512], P('expert', 'dp')
Inputs may be any that keep to these rules, and one draw needn't show every extreme that they name: `slot_row`: each source shard fills each of its slots with a token of that shard or leaves it empty; a token may fill several slots. `block_hot`: every expert group runs at least one block of the hot expert and at least one block of its own expert.
All inputs are finite; a program needn't handle non-finite values.
Results may differ from a plain program's by a relative error of at most 0.014.
Values may be sent and summed in bfloat16 or wider, within the bound.
No kernel may reach another device: no remote copies, remote signals or barrier semaphores. Data moves between devices by JAX's collectives and lax.ppermute only.
A program may use at most 192 MiB of HBM per device.

v0:
```python
import jax
import jax.numpy as jnp
from jax import lax
from jax.sharding import PartitionSpec as P

BLOCK = 128


def from_root(value, axis, source):
    kept = jnp.where(lax.axis_index(axis) == source, value, 0).astype(value.dtype)
    return lax.psum(kept, axis)


def local(tokens_t, slot_row, slot_gate, block_hot, hot_owner, w_in, w_out):
    slot_ids = slot_row[0]
    slot_weights = slot_gate[0]
    hot_flags = block_hot[0]
    num_blocks = hot_flags.shape[0]
    tok_local = tokens_t.shape[1]
    feature_rows = tokens_t.shape[0]
    width = w_in.shape[3]
    live_mask = (slot_ids >= 0).astype(tokens_t.dtype)
    row_index = jnp.maximum(slot_ids, 0)
    slot_total = slot_ids.shape[0]
    res_in = w_in[0].reshape(-1, width)
    root_index = hot_owner[0] % lax.axis_size("dp")
    hot_pair = (from_root(w_in, "dp", root_index), from_root(w_out, "dp", root_index))
    hot_in = hot_pair[0][0].reshape(-1, width)
    hot_out_full = hot_pair[1]
    empty_sum = jnp.zeros((res_in.shape[0], slot_total), jnp.float32)
    outgoing = jnp.take(tokens_t, row_index, axis=1) * live_mask[None, :]
    incoming = lax.all_to_all(outgoing, "dp", split_axis=1, concat_axis=1, tiled=True)
    shard_rows = lax.all_gather(incoming, "expert", axis=0, tiled=True)

    def up_add_block(j, running):
        block_cols = lax.dynamic_slice_in_dim(shard_rows, j * BLOCK, BLOCK, 1)
        product = lax.cond(
            hot_flags[j] > 0,
            lambda: jnp.dot(hot_in, block_cols, preferred_element_type=jnp.float32),
            lambda: jnp.dot(res_in, block_cols, preferred_element_type=jnp.float32),
        )
        previous = lax.dynamic_slice_in_dim(running, j * BLOCK, BLOCK, 1)
        return lax.dynamic_update_slice_in_dim(running, previous + product, j * BLOCK, 1)

    gate_up = lax.fori_loop(0, num_blocks, up_add_block, empty_sum)
    half_rows = gate_up.shape[0] // 2
    hidden = (jax.nn.silu(gate_up[:half_rows]) * gate_up[half_rows:]).astype(jnp.bfloat16)
    res_moved, hot_moved = (
        lax.all_to_all(w_out, "expert", split_axis=1, concat_axis=2, tiled=True),
        lax.all_to_all(hot_out_full, "expert", split_axis=1, concat_axis=2, tiled=True),
    )
    res_by_feat = res_moved[0]
    hot_by_feat = hot_moved[0]
    start_sum = jnp.zeros((feature_rows, slot_total), jnp.float32)
    piece = lax.all_gather(hidden, "expert", axis=0, tiled=True)
    count_rows = piece.shape[0]
    groups = count_rows // half_rows
    fold_res_cols = res_by_feat.reshape(feature_rows, groups, half_rows)
    fold_hot_cols = hot_by_feat.reshape(feature_rows, groups, half_rows)

    def fold_add_block(j, running):
        hidden_block = lax.dynamic_slice_in_dim(piece, j * BLOCK, BLOCK, 1).reshape(
            groups, half_rows, BLOCK
        )
        sums = lax.cond(
            hot_flags[j] > 0,
            lambda: jnp.einsum(
                "dgf,gfb->gdb", fold_hot_cols, hidden_block, preferred_element_type=jnp.float32
            ),
            lambda: jnp.einsum(
                "dgf,gfb->gdb", fold_res_cols, hidden_block, preferred_element_type=jnp.float32
            ),
        )
        rounded = jnp.sum(sums.astype(jnp.bfloat16).astype(jnp.float32), axis=0)
        previous = lax.dynamic_slice_in_dim(running, j * BLOCK, BLOCK, 1)
        return lax.dynamic_update_slice_in_dim(running, previous + rounded, j * BLOCK, 1)

    summed = lax.fori_loop(0, num_blocks, fold_add_block, start_sum)
    expert_out = summed.astype(jnp.bfloat16)
    returned = lax.all_to_all(expert_out, "dp", split_axis=1, concat_axis=1, tiled=True)
    choose = (slot_ids[:, None] == jnp.arange(tok_local, dtype=jnp.int32)[None, :]).astype(
        jnp.float32
    )
    choose = choose * slot_weights[:, None]
    choose_high = choose.astype(jnp.bfloat16)
    choose_low = (choose - choose_high.astype(jnp.float32)).astype(jnp.bfloat16)
    mixed = jnp.dot(returned, choose_high, preferred_element_type=jnp.float32)
    mixed = mixed + jnp.dot(returned, choose_low, preferred_element_type=jnp.float32)
    return mixed.astype(jnp.bfloat16)


def solution(mesh):
    return jax.shard_map(
        local,
        mesh=mesh,
        in_specs=(
            P("expert", "dp"),
            P("dp", None),
            P("dp", None),
            P("dp", None),
            P(),
            P("dp", None, "expert", None),
            P("dp", None, "expert"),
        ),
        out_specs=P("expert", "dp"),
        check_vma=False,
    )
```

profile of v0, /device:TPU:0, one launch (start us, length us, event | category | flops | bytes accessed | tf_op | source)
XLA Modules:
  0.0 689.5 jit_solution(4974403470930709530)
XLA Ops:
  8.1 11.9 %fusion.13 = (bf16[1,7168,256]{2,0,1:T(2,128)(2,1)}, bf16[1,7168,256]{2,0,1:T(2,128)(2,1)}) fusion(bf16[1,7168,256]{2,1,0:T(8,128)(2,1)} %param.21, pred[]{:T(512)S(6)} %eq.10), kind=kLoop, calls=%fused_computation.31 | loop fusion | flops 1835008 | bytes 11010049 | tf_op args[6]
  29.1 47.0 %all_to_all.51 = bf16[896,4,256]{0,2,1:T(8,128)(2,1)S(1)} all-to-all(bf16[896,4,256]{0,2,1:T(8,128)(2,1)S(1)} %select_multiply_fusion), channel_id=1, replica_groups=mesh['expert'=8,'dp'=4] {'dp'}, dimensions={1} | all-to-all | bytes 3670016 | tf_op jit(solution)/shard_map/all_to_all | solution.py:32
  79.1 38.4 %reduce.4 = bf16[7168,256]{1,0:T(8,128)(2,1)} reduce(bf16[7168,1,256]{2,1,0:T(2,128)(2,1)} %bitcast.54, bf16[]{:T(256)} %broadcast.60), dimensions={1}, to_apply=%bitcast.26.reduce_sub_computation | reduce | bytes 7340034
  117.5 6.8 reshape.71
  124.3 5.9 all-to-all-start.1
  130.4 170.1 %all-reduce.3.cloned.1.call-done = (bf16[512,7168]{1,0:T(8,128)(2,1)}, bf16[1,7168,256]{2,0,1:T(2,128)(2,1)}) async-done(((bf16[512,7168]{1,0:T(8,128)(2,1)}, bf16[1,7168,256]{2,0,1:T(2,128)(2,1)}), (bf16[512,7168]{1,0:T(8,128)(2,1)}, bf16[1,7168,256]{2,0,1:T(2,128)(2,1)})) %all-reduce.3.cloned.1.call-update) | async-done | bytes 11010064 | tf_op jit(solution)/shard_map/psum | solution.py:11
  300.6 49.0 %all-gather.3.cloned.1.call-done = bf16[7168,1024]{1,0:T(8,128)(2,1)} async-done(((bf16[896,1024]{1,0:T(8,128)(2,1)}), bf16[7168,1024]{1,0:T(8,128)(2,1)}) %all-gather.3.cloned.1.call-update) | async-done | bytes 14680080 | tf_op jit(solution)/shard_map/all_gather | solution.py:33
  349.8 65.3 %while.26 = (s32[]{:T(128)}, f32[512,1024]{1,0:T(8,128)S(1)}, s32[8]{0:T(128)S(1)}, bf16[7168,1024]{1,0:T(8,128)(2,1)}, bf16[512,7168]{1,0:T(8,128)(2,1)}, /*ind...) while((s32[]{:T(128)}, f32[512,1024]{1,0:T(8,128)S(1)}, ...), condition=%wide.region_4.5_spmd, body=%wide.region_1.4_spmd.sunk | while | flops 939589632 | bytes 13893861 | solution.py:45
  352.7 5.2 conditional.4
  352.7 5.2 fusion.14
  360.8 5.2 conditional.4
  360.9 5.2 fusion.15
  369.0 5.2 conditional.4
  369.0 5.2 fusion.14
  377.2 5.2 conditional.4
  377.2 5.2 fusion.15
  385.3 5.2 conditional.4
  385.4 5.2 fusion.14
  393.5 5.2 conditional.4
  393.5 5.2 fusion.14
  401.7 5.2 conditional.4
  409.8 5.2 conditional.4
  409.8 5.2 fusion.14
  416.2 38.3 %reduce.5 = bf16[7168,256]{1,0:T(8,128)(2,1)} reduce(bf16[7168,1,256]{2,1,0:T(2,128)(2,1)} %bitcast.60, bf16[]{:T(256)} %broadcast.60), dimensions={1}, to_apply=%bitcast.28.reduce_sub_computation | reduce | bytes 7340034
  454.5 6.7 reshape.73
  465.9 8.3 %reshape.72 = bf16[7168,1,256]{2,1,0:T(2,128)(2,1)} reshape(bf16[8,2,114688]{2,1,0:T(2,128)(2,1)} %all-to-all-done.1) | data formatting | bytes 7340032
  474.2 5.6 copy.25
  479.8 83.8 %all-to-all-done.2 = bf16[8,2,114688]{2,1,0:T(2,128)(2,1)} async-done(((bf16[8,2,114688]{2,1,0:T(2,128)(2,1)}), bf16[8,2,114688]{2,1,0:T(2,128)(2,1)}, u32[]{:S(2)}, u32[]{:S(2)}) %all-to-all-start.2) | async-done | bytes 3670048 | tf_op jit(solution)/shard_map/all_to_all | solution.py:50
  563.6 8.3 %reshape.74 = bf16[7168,1,256]{2,1,0:T(2,128)(2,1)} reshape(bf16[8,2,114688]{2,1,0:T(2,128)(2,1)} %all-to-all-done.2) | data formatting | bytes 7340032
  571.8 5.5 copy.26
  579.4 64.8 %while.27 = (s32[]{:T(128)}, f32[896,1024]{0,1:T(8,128)}, s32[8]{0:T(128)S(1)}, bf16[2048,1024]{1,0:T(8,128)(2,1)}, bf16[896,8,256]{2,0,1:T(8,128)(2,1)}, /*inde...) while((s32[]{:T(128)}, f32[896,1024]{0,1:T(8,128)}, ...), condition=%wide.region_10.11_spmd, body=%wide.region_6.10_spmd.sunk | while | flops 471597056 | bytes 14418153 | solution.py:78
  650.4 26.1 %all_to_all.52 = bf16[896,4,256]{2,0,1:T(8,128)(2,1)} all-to-all(bf16[896,4,256]{2,0,1:T(8,128)(2,1)S(1)} %copy.19), channel_id=1, replica_groups=mesh['expert'=8,'dp'=4] {'dp'}, dimensions={1} | all-to-all | bytes 3670016 | tf_op jit(solution)/shard_map/all_to_all | solution.py:80
  (144 shorter events, 140.4 us)
Async XLA Ops:
  7.4 293.2 %all-reduce.3.cloned.1.call-start = ((), (), s32[]{:S(2)}) async-start(), calls=%async_computation.6 | async-start | bytes 29360128 | tf_op jit(solution)/shard_map/psum | solution.py:11
  8.0 11.9 %copy-start = (bf16[1,2,256,7168]{3,2,1,0:T(8,128)(2,1)S(1)}, bf16[1,2,256,7168]{3,2,1,0:T(8,128)(2,1)}, u32[]{:S(2)}) copy-start(bf16[1,2,256,7168]{3,2,1,0:T(8,128)(2,1)} %param.20) | copy-start | bytes 22020100
  23.4 0.9 copy-start.1
  23.4 1.1 copy-start.2
  23.4 326.1 %all-gather.3.cloned.1.call-start = ((), (), s32[]{:S(2)}) async-start(), calls=%async_computation.4 | async-start | bytes 16515072 | tf_op jit(solution)/shard_map/all_gather | solution.py:33
  124.2 225.5 %copy-start.4 = (s32[1,8]{1,0:T(1,128)S(1)}, s32[1,8]{1,0:T(1,128)}, u32[]{:S(2)}) copy-start(s32[1,8]{1,0:T(1,128)} %param.18) | copy-start | bytes 100
  124.3 337.0 %all-to-all-start.1 = ((bf16[8,2,114688]{2,1,0:T(2,128)(2,1)}), bf16[8,2,114688]{2,1,0:T(2,128)(2,1)}, u32[]{:S(2)}, u32[]{:S(2)}) async-start(bf16[8,2,114688]{2,1,0:T(2,128)(2,1)} %reshape.71), calls=%async_computation.1 | async-start | bytes 7340032 | tf_op jit(solution)/shard_map/all_to_all | solution.py:49
  130.2 447.1 %all-gather.5.cloned.1.call-start = ((), (), s32[]{:S(2)}) async-start(), calls=%async_computation.5 | async-start | bytes 4718592 | tf_op jit(solution)/shard_map/all_gather | solution.py:55
  461.2 102.3 %all-to-all-start.2 = ((bf16[8,2,114688]{2,1,0:T(2,128)(2,1)}), bf16[8,2,114688]{2,1,0:T(2,128)(2,1)}, u32[]{:S(2)}, u32[]{:S(2)}) async-start(bf16[8,2,114688]{2,1,0:T(2,128)(2,1)} %reshape.73), calls=%async_computation.2 | async-start | bytes 7340032 | tf_op jit(solution)/shard_map/all_to_all | solution.py:50
  650.4 28.9 %copy-start.3 = (f32[1,1024]{1,0:T(1,128)S(1)}, f32[1,1024]{1,0:T(1,128)}, u32[]{:S(2)}) copy-start(f32[1,1024]{1,0:T(1,128)} %param.17) | copy-start | bytes 12292
Sparse Core Ops, SparseCore 0:
  23.6 276.9 all-reduce.2
Sparse Core Ops, SparseCore 1:
  78.6 270.8 all-gather.2
  416.3 97.5 all-gather.4
where the time goes:
time: 692 us; the launch traced here: 689 us
  waiting for transfers between devices  303 us (44%)
  local copies, waits for them, and re-layouts  106 us (15%)
  other arithmetic  100 us (14%)
  blocking collectives  73 us (11%)
  matrix products  69.2 us (10%)
  between operations  15.7 us (2%)
  loops' own time  11.2 us (2%)
  starting transfers between devices  10.9 us (2%)
    psum x1, waiting for transfers between devices, from_root(): return lax.psum(kept, axis)  170 us
    unnamed x3, other arithmetic  88.7 us
    all_to_all x1, waiting for transfers between devices, local(): lax.all_to_all(hot_out_full, 'expert', split_axis=1, concat_axis=2, tiled...  83.8 us
    all_gather x1, waiting for transfers between devices, local(): shard_rows = lax.all_gather(incoming, 'expert', axis=0, tiled=True)  49 us
    all_to_all x1, blocking collectives, local(): lax.all_to_all(outgoing, 'dp', split_axis=1, concat_axis=1, tiled=True)  47 us
    unnamed x18, local copies, waits for them, and re-layouts  42.6 us
    all_to_all x1, blocking collectives, local(): lax.all_to_all(expert_out, 'dp', split_axis=1, concat_axis=1, tiled=True)  26.1 us
    dot_general x5, matrix products, up_add_block(): jnp.dot(res_in, block_cols, preferred_element_type=jnp.float32)  25.8 us
  transfers between devices with their start and end apart: 5, of which 3 were waited for; matrix products, arithmetic and copies ran while one was open for 27% of the time, Pallas kernels for 0%

commit v1 on v0

--- a/solution.py
+++ b/solution.py
@@ -30,7 +30,16 @@
     empty_sum = jnp.zeros((res_in.shape[0], slot_total), jnp.float32)
     outgoing = jnp.take(tokens_t, row_index, axis=1) * live_mask[None, :]
     incoming = lax.all_to_all(outgoing, "dp", split_axis=1, concat_axis=1, tiled=True)
-    shard_rows = lax.all_gather(incoming, "expert", axis=0, tiled=True)
+    ways = lax.axis_size("expert")
+    up = [(d, (d + 1) % ways) for d in range(ways)]
+    down = [(d, (d - 1) % ways) for d in range(ways)]
+    earlier, later = ([incoming], [incoming])
+    for _ in range(ways // 2):
+        earlier.append(lax.ppermute(earlier[-1], "expert", up))
+    for _ in range((ways - 1) // 2):
+        later.append(lax.ppermute(later[-1], "expert", down))
+    line = jnp.concatenate([*earlier[::-1], *later[1:]], axis=0)
+    shard_rows = jnp.roll(line, (lax.axis_index("expert") - ways // 2) * incoming.shape[0], axis=0)
 
     def up_add_block(j, running):
         block_cols = lax.dynamic_slice_in_dim(shard_rows, j * BLOCK, BLOCK, 1)

time: 692 us -> 851 us (1.23)
  starting transfers between devices: 10.9 us -> 89.1 us
  waiting for transfers between devices: 303 us -> 372 us
  local copies, waits for them, and re-layouts: 106 us -> 138 us
  blocking collectives: 73 us -> 53.1 us
    ppermute x0 -> x7, waiting for transfers between devices: none -> 153 us  [the longest x4 153 us: local(): earlier.append(lax.ppermute(earlier[-1], 'expert', up))]
    ppermute x0 -> x7, starting transfers between devices: none -> 78.9 us  [the longest x3 71.8 us: local(): later.append(lax.ppermute(later[-1], 'expert', down))]
    all_gather x1 -> x0, waiting for transfers between devices: 49 us -> none  [local(): shard_rows = lax.all_gather(incoming, 'expert', axis=0, tiled=True)]
    psum x1, waiting for transfers between devices: 170 us -> 134 us  [from_root(): return lax.psum(kept, axis)]
    unnamed x18 -> x29, local copies, waits for them, and re-layouts: 42.6 us -> 64.6 us
    all_to_all x1, blocking collectives: 47 us -> 27 us  [local(): lax.all_to_all(outgoing, 'dp', split_axis=1, concat_axis=1, tiled=True)]
  transfers between devices with their start and end apart: 5 -> 11, of which waited for: 3 -> 5; matrix products, arithmetic and copies ran while one was open for 27% -> 27% of each run, Pallas kernels for 0% -> 0%
where the time goes in v1:
time: 851 us; the launch traced here: 847 us
  waiting for transfers between devices  372 us (44%)
  local copies, waits for them, and re-layouts  138 us (16%)
  other arithmetic  102 us (12%)
  starting transfers between devices  89.1 us (10%)
  matrix products  69.2 us (8%)
  blocking collectives  53.1 us (6%)
  between operations  14.3 us (2%)
  loops' own time  9.98 us (1%)
    ppermute x4, waiting for transfers between devices, local(): earlier.append(lax.ppermute(earlier[-1], 'expert', up))  153 us
    psum x1, waiting for transfers between devices, from_root(): return lax.psum(kept, axis)  134 us
    unnamed x3, other arithmetic  88.5 us
    all_to_all x1, waiting for transfers between devices, local(): lax.all_to_all(hot_out_full, 'expert', split_axis=1, concat_axis=2, tiled...  85.1 us
    ppermute x3, starting transfers between devices, local(): later.append(lax.ppermute(later[-1], 'expert', down))  71.8 us
    unnamed x29, local copies, waits for them, and re-layouts  64.6 us
    all_to_all x1, blocking collectives, local(): lax.all_to_all(outgoing, 'dp', split_axis=1, concat_axis=1, tiled=True)  27 us
    all_to_all x1, blocking collectives, local(): lax.all_to_all(expert_out, 'dp', split_axis=1, concat_axis=1, tiled=True)  26.1 us
  transfers between devices with their start and end apart: 11, of which 5 were waited for; matrix products, arithmetic and copies ran while one was open for 27% of the time, Pallas kernels for 0%

profile of v1, /device:TPU:0, one launch (start us, length us, event | category | flops | bytes accessed | tf_op | source)
XLA Modules:
  0.0 847.4 jit_solution(7725136745419476184)
XLA Ops:
  14.2 27.0 %all_to_all.51 = bf16[896,4,256]{0,2,1:T(8,128)(2,1)} all-to-all(bf16[896,4,256]{0,2,1:T(8,128)(2,1)S(1)} %select_multiply_fusion), channel_id=1, replica_groups=mesh['expert'=8,'dp'=4] {'dp'}, dimensions={1} | all-to-all | bytes 3670016 | tf_op jit(solution)/shard_map/all_to_all | solution.py:32
  46.3 42.8 %collective-permute-done = bf16[896,1024]{1,0:T(8,128)(2,1)} collective-permute-done((bf16[896,1024]{1,0:T(8,128)(2,1)S(1)}, bf16[896,1024]{1,0:T(8,128)(2,1)}, u32[]{:S(2)}, u32[]{:S(2)}) %collective-permute-start) | collective-permute-done | bytes 1835040 | tf_op jit(solution)/shard_map/ppermute | solution.py:38
  94.5 72.8 %collective-permute-done.1 = bf16[896,1024]{1,0:T(8,128)(2,1)} collective-permute-done((bf16[896,1024]{1,0:T(8,128)(2,1)}, bf16[896,1024]{1,0:T(8,128)(2,1)}, u32[]{:S(2)}, u32[]{:S(2)}) %collective-permute-start.1) | collective-permute-done | bytes 1835040 | tf_op jit(solution)/shard_map/ppermute | solution.py:38
  169.8 11.8 %fusion.13 = (bf16[1,7168,256]{2,0,1:T(2,128)(2,1)}, bf16[1,7168,256]{2,0,1:T(2,128)(2,1)}) fusion(bf16[1,7168,256]{2,1,0:T(8,128)(2,1)} %param.21, pred[]{:T(512)S(6)} %eq.22), kind=kLoop, calls=%fused_computation.48 | loop fusion | flops 1835008 | bytes 11010049 | tf_op args[6]
  181.6 28.4 %collective-permute-start.5 = (bf16[896,1024]{1,0:T(8,128)(2,1)}, bf16[896,1024]{1,0:T(8,128)(2,1)}, u32[]{:S(2)}, u32[]{:S(2)}) collective-permute-start(bf16[896,1024]{1,0:T(8,128)(2,1)} %collective-permute-done.4), channel_id=1, source_target_pairs={{0,28},{4,0},{8,4},{12,8},{16,12},{20,16},{24,20},{28,24},{1,29},{... | collective-permute-start | bytes 5505032 | tf_op jit(solution)/shard_map/ppermute | solution.py:40
  210.0 37.2 %collective-permute-done.2 = bf16[896,1024]{1,0:T(8,128)(2,1)} collective-permute-done((bf16[896,1024]{1,0:T(8,128)(2,1)}, bf16[896,1024]{1,0:T(8,128)(2,1)}, u32[]{:S(2)}, u32[]{:S(2)}) %collective-permute-start.2) | collective-permute-done | bytes 1835040 | tf_op jit(solution)/shard_map/ppermute | solution.py:38
  253.1 38.6 %collective-permute-start.6 = (bf16[896,1024]{1,0:T(8,128)(2,1)}, bf16[896,1024]{1,0:T(8,128)(2,1)}, u32[]{:S(2)}, u32[]{:S(2)}) collective-permute-start(bf16[896,1024]{1,0:T(8,128)(2,1)} %collective-permute-done.5), channel_id=1, source_target_pairs={{0,28},{4,0},{8,4},{12,8},{16,12},{20,16},{24,20},{28,24},{1,29},{... | collective-permute-start | bytes 5505032 | tf_op jit(solution)/shard_map/ppermute | solution.py:40
  292.2 38.3 %reduce.4 = bf16[7168,256]{1,0:T(8,128)(2,1)} reduce(bf16[7168,1,256]{2,1,0:T(2,128)(2,1)} %bitcast.54, bf16[]{:T(256)} %broadcast.60), dimensions={1}, to_apply=%bitcast.26.reduce_sub_computation | reduce | bytes 7340034
  330.6 6.7 reshape.71
  365.7 7.8 constant_dynamic-slice_fusion.3
  373.6 133.7 %all-reduce.3.cloned.1.call-done = (bf16[512,7168]{1,0:T(8,128)(2,1)}, bf16[1,7168,256]{2,0,1:T(2,128)(2,1)}) async-done(((bf16[512,7168]{1,0:T(8,128)(2,1)}, bf16[1,7168,256]{2,0,1:T(2,128)(2,1)}), (bf16[512,7168]{1,0:T(8,128)(2,1)}, bf16[1,7168,256]{2,0,1:T(2,128)(2,1)})) %all-reduce.3.cloned.1.call-update) | async-done | bytes 11010064 | tf_op jit(solution)/shard_map/psum | solution.py:11
  507.5 64.5 %while.26 = (s32[]{:T(128)}, f32[512,1024]{1,0:T(8,128)S(1)}, s32[8]{0:T(128)S(1)}, bf16[7168,1024]{1,0:T(8,128)(2,1)}, bf16[512,7168]{1,0:T(8,128)(2,1)}, /*ind...) while((s32[]{:T(128)}, f32[512,1024]{1,0:T(8,128)S(1)}, ...), condition=%wide.region_4.5_spmd, body=%wide.region_1.4_spmd.sunk | while | flops 939589632 | bytes 13893861 | solution.py:54
  510.3 5.2 conditional.4
  510.3 5.2 fusion.14
  518.4 5.2 conditional.4
  526.4 5.2 conditional.4
  534.5 5.2 conditional.4
  542.6 5.2 conditional.4
  542.6 5.2 fusion.14
  550.6 5.2 conditional.4
  558.7 5.2 conditional.4
  566.8 5.2 conditional.4
  573.2 38.4 %reduce.5 = bf16[7168,256]{1,0:T(8,128)(2,1)} reduce(bf16[7168,1,256]{2,1,0:T(2,128)(2,1)} %bitcast.60, bf16[]{:T(256)} %broadcast.60), dimensions={1}, to_apply=%bitcast.28.reduce_sub_computation | reduce | bytes 7340034
  611.6 6.7 reshape.73
  618.3 5.5 all-to-all-start.2
  623.8 8.3 reshape.72
  632.0 5.5 copy.25
  637.5 85.1 %all-to-all-done.2 = bf16[8,2,114688]{2,1,0:T(2,128)(2,1)} async-done(((bf16[8,2,114688]{2,1,0:T(2,128)(2,1)}), bf16[8,2,114688]{2,1,0:T(2,128)(2,1)}, u32[]{:S(2)}, u32[]{:S(2)}) %all-to-all-start.2) | async-done | bytes 3670048 | tf_op jit(solution)/shard_map/all_to_all | solution.py:59
  722.6 8.2 reshape.74
  730.9 5.6 copy.26
  738.6 64.0 %while.27 = (s32[]{:T(128)}, f32[896,1024]{0,1:T(8,128)}, s32[8]{0:T(128)S(1)}, bf16[2048,1024]{1,0:T(8,128)(2,1)}, bf16[896,8,256]{2,0,1:T(8,128)(2,1)}, /*inde...) while((s32[]{:T(128)}, f32[896,1024]{0,1:T(8,128)}, ...), condition=%wide.region_10.11_spmd, body=%wide.region_6.10_spmd.sunk | while | flops 471597056 | bytes 14418153 | solution.py:87
  808.9 26.1 %all_to_all.52 = bf16[896,4,256]{2,0,1:T(8,128)(2,1)} all-to-all(bf16[896,4,256]{2,0,1:T(8,128)(2,1)S(1)} %copy.19), channel_id=1, replica_groups=mesh['expert'=8,'dp'=4] {'dp'}, dimensions={1} | all-to-all | bytes 3670016 | tf_op jit(solution)/shard_map/all_to_all | solution.py:89
  (168 shorter events, 203.6 us)
Async XLA Ops:
  6.5 500.7 %all-reduce.3.cloned.1.call-start = ((), (), s32[]{:S(2)}) async-start(), calls=%async_computation.5 | async-start | bytes 29360128 | tf_op jit(solution)/shard_map/psum | solution.py:11
  44.1 44.9 %collective-permute-start = (bf16[896,1024]{1,0:T(8,128)(2,1)S(1)}, bf16[896,1024]{1,0:T(8,128)(2,1)}, u32[]{:S(2)}, u32[]{:S(2)}) collective-permute-start(bf16[896,1024]{1,0:T(8,128)(2,1)S(1)} %copy.21), channel_id=1, source_target_pairs={{0,4},{4,8},{8,12},{12,16},{16,20},{20,24},{24,28},{28,0},{1,5},{5... | collective-permute-start | bytes 5505032 | tf_op jit(solution)/shard_map/ppermute | solution.py:38
  89.0 78.3 %collective-permute-start.1 = (bf16[896,1024]{1,0:T(8,128)(2,1)}, bf16[896,1024]{1,0:T(8,128)(2,1)}, u32[]{:S(2)}, u32[]{:S(2)}) collective-permute-start(bf16[896,1024]{1,0:T(8,128)(2,1)} %collective-permute-done), channel_id=1, source_target_pairs={{0,4},{4,8},{8,12},{12,16},{16,20},{20,24},{24,28},{28,0},{1,5},{5... | collective-permute-start | bytes 5505032 | tf_op jit(solution)/shard_map/ppermute | solution.py:38
  89.7 91.8 %collective-permute-start.4 = (bf16[896,1024]{1,0:T(8,128)(2,1)S(1)}, bf16[896,1024]{1,0:T(8,128)(2,1)}, u32[]{:S(2)}, u32[]{:S(2)}) collective-permute-start(bf16[896,1024]{1,0:T(8,128)(2,1)S(1)} %copy.21), channel_id=1, source_target_pairs={{0,28},{4,0},{8,4},{12,8},{16,12},{20,16},{24,20},{28,24},{1,29},{... | collective-permute-start | bytes 5505032 | tf_op jit(solution)/shard_map/ppermute | solution.py:40
  167.3 79.9 %collective-permute-start.2 = (bf16[896,1024]{1,0:T(8,128)(2,1)}, bf16[896,1024]{1,0:T(8,128)(2,1)}, u32[]{:S(2)}, u32[]{:S(2)}) collective-permute-start(bf16[896,1024]{1,0:T(8,128)(2,1)} %collective-permute-done.1), channel_id=1, source_target_pairs={{0,4},{4,8},{8,12},{12,16},{16,20},{20,24},{24,28},{28,0},{1,5},{5... | collective-permute-start | bytes 5505032 | tf_op jit(solution)/shard_map/ppermute | solution.py:38
  181.6 71.5 %collective-permute-start.5 = (bf16[896,1024]{1,0:T(8,128)(2,1)}, bf16[896,1024]{1,0:T(8,128)(2,1)}, u32[]{:S(2)}, u32[]{:S(2)}) collective-permute-start(bf16[896,1024]{1,0:T(8,128)(2,1)} %collective-permute-done.4), channel_id=1, source_target_pairs={{0,28},{4,0},{8,4},{12,8},{16,12},{20,16},{24,20},{28,24},{1,29},{... | collective-permute-start | bytes 5505032 | tf_op jit(solution)/shard_map/ppermute | solution.py:40
  247.2 94.9 %collective-permute-start.3 = (bf16[896,1024]{1,0:T(8,128)(2,1)}, bf16[896,1024]{1,0:T(8,128)(2,1)}, u32[]{:S(2)}, u32[]{:S(2)}) collective-permute-start(bf16[896,1024]{1,0:T(8,128)(2,1)} %collective-permute-done.2), channel_id=1, source_target_pairs={{0,4},{4,8},{8,12},{12,16},{16,20},{20,24},{24,28},{28,0},{1,5},{5... | collective-permute-start | bytes 5505032 | tf_op jit(solution)/shard_map/ppermute | solution.py:38
  253.1 99.2 %collective-permute-start.6 = (bf16[896,1024]{1,0:T(8,128)(2,1)}, bf16[896,1024]{1,0:T(8,128)(2,1)}, u32[]{:S(2)}, u32[]{:S(2)}) collective-permute-start(bf16[896,1024]{1,0:T(8,128)(2,1)} %collective-permute-done.5), channel_id=1, source_target_pairs={{0,28},{4,0},{8,4},{12,8},{16,12},{20,16},{24,20},{28,24},{1,29},{... | collective-permute-start | bytes 5505032 | tf_op jit(solution)/shard_map/ppermute | solution.py:40
  337.3 281.0 %all-to-all-start.1 = ((bf16[8,2,114688]{2,1,0:T(2,128)(2,1)}), bf16[8,2,114688]{2,1,0:T(2,128)(2,1)}, u32[]{:S(2)}, u32[]{:S(2)}) async-start(bf16[8,2,114688]{2,1,0:T(2,128)(2,1)} %reshape.71), calls=%async_computation.1 | async-start | bytes 7340032 | tf_op jit(solution)/shard_map/all_to_all | solution.py:58
  341.8 394.6 %all-gather.2.cloned.1.call-start = ((), (), s32[]{:S(2)}) async-start(), calls=%async_computation.4 | async-start | bytes 4718592 | tf_op jit(solution)/shard_map/all_gather | solution.py:64
  365.7 141.8 %copy-start.2 = (s32[1,8]{1,0:T(1,128)S(1)}, s32[1,8]{1,0:T(1,128)}, u32[]{:S(2)}) copy-start(s32[1,8]{1,0:T(1,128)} %param.18) | copy-start | bytes 100
  618.3 104.3 %all-to-all-start.2 = ((bf16[8,2,114688]{2,1,0:T(2,128)(2,1)}), bf16[8,2,114688]{2,1,0:T(2,128)(2,1)}, u32[]{:S(2)}, u32[]{:S(2)}) async-start(bf16[8,2,114688]{2,1,0:T(2,128)(2,1)} %reshape.73), calls=%async_computation.2 | async-start | bytes 7340032 | tf_op jit(solution)/shard_map/all_to_all | solution.py:59
  808.9 29.0 %copy-start = (s32[1,1024]{1,0:T(1,128)S(1)}, s32[1,1024]{1,0:T(1,128)}, u32[]{:S(2)}) copy-start(s32[1,1024]{1,0:T(1,128)} %param.16) | copy-start | bytes 12292
  808.9 29.0 %copy-start.1 = (f32[1,1024]{1,0:T(1,128)S(1)}, f32[1,1024]{1,0:T(1,128)}, u32[]{:S(2)}) copy-start(f32[1,1024]{1,0:T(1,128)} %param.17) | copy-start | bytes 12292
Sparse Core Ops, SparseCore 0:
  253.2 254.0 all-reduce.2
  573.3 99.5 all-gather.1
